TPU v7x, 32 devices: a whole 2x2x4 slice. The times are simulated.
32 devices in a mesh: team: 8 (over z, core), member: 4 (over y, x).
Axes of the slice: x: 2, y: 2, z: 4, core: 2. Of those that a mesh axis runs over, the one named last changes fastest.
Arguments:
- state_start: float32 [24, 512, 512], P(None, 'team', 'member'), may hold values from -6 to 6
- state_section: float32 [24, 512, 512], P(None, 'team', 'member'), may hold values from -6 to 6
- velocity: float32 [2, 512, 512], P(None, 'team', 'member'), may hold values from -3 to 3
- diffusivity: float32 [24], replicated, may hold values from 0.05 to 0.5
- flame_cells: int32 [32, 128], P(('team', 'member')), may hold values from 0 to 8191, as said below
- block_team: int32 [32, 1], replicated, may hold values from 0 to 7; in each aligned block of 4 rows (0 to 3, 4 to 7, ...) at most 2 rows name the same one
- w_in: bfloat16 [8, 4, 1600, 24], P('team', 'member'), may hold values from -1.25 to 1.25
- w_mid: bfloat16 [8, 4, 800, 1600], P('team', 'member'), may hold values from -0.15625 to 0.15625
- w_low: bfloat16 [8, 4, 400, 800], P('team', 'member'), may hold values from -0.21875 to 0.21875
- w_out: bfloat16 [8, 4, 24, 400], P('team', 'member'), may hold values from -0.3125 to 0.3125
Outputs:
- source_rates: float32 [24, 512, 512], P(None, 'team', 'member')
- new_state: float32 [24, 512, 512], P(None, 'team', 'member')
Inputs may be any that keep to these rules, and one draw needn't show every extreme that they name: `flame_cells`: the 128 entries of the rows of one device (rows d * 1 to d + 1 - 1) are distinct cells of that device's tile, given as i * 128 + j. `block_team`: in each aligned block of 4 rows (the flame blocks of one index of team) no regime appears more than 2 times.
All inputs are finite; a program needn't handle non-finite values.
Results may differ from a plain program's by a relative error of at most 0.0017.
The roundings to bfloat16 on the way count: a program that leaves them out, or rounds other values in their place, can miss the bound.
Values may be sent and summed in bfloat16 or wider, within the bound.
A program may use at most 64 MiB of HBM per device.

v0:
```python
import functools

import jax
import jax.numpy as jnp
from jax import lax
from jax.experimental import pallas as pl
from jax.experimental.pallas import tpu as pltpu
from jax.sharding import PartitionSpec as P

CAP = 2
TIME_STEP = 0.25
GRANT = 16 << 20
MESH = pl.DeviceIdType.MESH
VMEM = pltpu.VMEM
F32 = jnp.float32
BF16 = jnp.bfloat16


def spread_order(count):
    order = []
    for step in range(1, count // 2 + 1):
        order.append(step)
        if count - step != step:
            order.append(count - step)
    return order


def split_cells(cells, rows_y):
    shift = rows_y.bit_length() - 1
    assert rows_y == 1 << shift
    return cells >> shift, cells & (rows_y - 1)


def row_mask(cells_x, rows_x):
    count = cells_x.shape[1]
    return lax.broadcasted_iota(jnp.int32, (rows_x, count), 0) == cells_x


def silu(x):
    half = 0.5 * x
    return half + half * jnp.tanh(half)


def greet(team, member, teams, members):
    barrier = pltpu.get_barrier_semaphore()
    for d in range(1, teams):
        pl.semaphore_signal(
            barrier, inc=1, device_id=(lax.rem(team + d, teams), member), device_id_type=MESH
        )
    for e in range(1, members):
        pl.semaphore_signal(
            barrier, inc=1, device_id=(team, lax.rem(member + e, members)), device_id_type=MESH
        )
    return barrier


def share_kernel(
    teams,
    members,
    section_ref,
    cells_ref,
    blocks_ref,
    halo_x_ref,
    halo_y_ref,
    edge_x,
    edge_y,
    send_t,
    recv_t,
    send_m,
    recv_m,
    send_h,
    recv_h,
):
    team = lax.axis_index("team")
    member = lax.axis_index("member")
    barrier = greet(team, member, teams, members)
    fields, rows_x, rows_y = section_ref.shape
    cells_x, cells_y = split_cells(cells_ref[...], rows_y)
    count = cells_x.shape[1]
    pick_y = (lax.broadcasted_iota(jnp.int32, (rows_y, count), 0) == cells_y).astype(F32)
    pick_x = row_mask(cells_x, rows_x)
    flat = section_ref[...].reshape(fields * rows_x, rows_y).astype(BF16)
    taken = jnp.dot(flat, pick_y.astype(BF16), preferred_element_type=F32)
    taken = taken.reshape(fields, rows_x, count)
    own = jnp.sum(jnp.where(pick_x[None], taken, 0.0), axis=1)
    blocks_ref[member, team] = own.astype(BF16)
    edge_x[0] = section_ref[:, rows_x - 1, :].astype(BF16)
    edge_x[1] = section_ref[:, 0, :].astype(BF16)
    lanes = lax.broadcasted_iota(jnp.int32, (rows_x, rows_y), 1)
    low = jnp.zeros((rows_x, rows_y), F32)
    high = jnp.zeros((rows_x, rows_y), F32)
    for f in range(fields):
        plane = section_ref[f]
        here = lanes == f
        high = jnp.where(here, pltpu.roll(plane, (f + 1) % rows_y, 1), high)
        low = jnp.where(here, pltpu.roll(plane, f, 1) if f else plane, low)
    edge_y[0] = high.astype(BF16)
    edge_y[1] = low.astype(BF16)
    pl.semaphore_wait(barrier, teams + members - 2)

    started = []
    t_copies = {}
    for d in spread_order(teams):
        copy = pltpu.make_async_remote_copy(
            src_ref=blocks_ref.at[member, team],
            dst_ref=blocks_ref.at[member, team],
            send_sem=send_t.at[d],
            recv_sem=recv_t.at[d],
            device_id=(lax.rem(team + d, teams), member),
            device_id_type=MESH,
        )
        copy.start()
        t_copies[d] = copy

    def forward(d):
        source = lax.rem(team - d + teams, teams)
        for e in range(1, members):
            copy = pltpu.make_async_remote_copy(
                src_ref=blocks_ref.at[member, source],
                dst_ref=blocks_ref.at[member, source],
                send_sem=send_m.at[d, e],
                recv_sem=recv_m.at[d, e],
                device_id=(team, lax.rem(member + e, members)),
                device_id_type=MESH,
            )
            copy.start()
            started.append(copy)

    forward(0)
    halos = []
    for k, (step, edge, halo, along) in enumerate(
        (
            (1, edge_x.at[0], halo_x_ref.at[0], "team"),
            (-1, edge_x.at[1], halo_x_ref.at[1], "team"),
            (1, edge_y.at[0], halo_y_ref.at[0], "member"),
            (-1, edge_y.at[1], halo_y_ref.at[1], "member"),
        )
    ):
        if along == "team":
            device = (lax.rem(team + step + teams, teams), member)
        else:
            device = (team, lax.rem(member + step + members, members))
        copy = pltpu.make_async_remote_copy(
            src_ref=edge,
            dst_ref=halo,
            send_sem=send_h.at[k],
            recv_sem=recv_h.at[k],
            device_id=device,
            device_id_type=MESH,
        )
        copy.start()
        halos.append(copy)
    for d in spread_order(teams):
        t_copies[d].wait_recv()
        forward(d)
    for copy in started + halos:
        copy.wait()
    for d in spread_order(teams):
        t_copies[d].wait_send()


def network_kernel(
    teams,
    members,
    team_of,
    blocks_ref,
    w_in,
    w_mid,
    w_low,
    w_out,
    slots_ref,
    first_weight,
    hidden_one,
    hidden_two,
    hidden_three,
    pick,
    place,
):
    team = lax.axis_index("team")
    fields, count = slots_ref.shape[1:]
    slots_ref[...] = jnp.zeros_like(slots_ref)

    def scan_team(p, found):
        seen = jnp.int32(0)
        for q in range(members):
            mine = (team_of[p * members + q] == team).astype(jnp.int32)
            pick[found] = q * teams + p
            place[found] = p * CAP + seen
            found = found + mine
            seen = seen + mine
        return found

    first_weight[0, 0] = w_in[0, 0].T
    found = lax.fori_loop(0, teams, scan_team, jnp.int32(0))
    last = jnp.maximum(found - 1, 0)
    pick[found] = pick[last]
    place[found] = place[last]

    def layer(weight, source, target, rows):
        total = weight.shape[2]
        start = 0
        while start < total:
            size = min(rows, total - start)
            span = pl.ds(start, size)
            out = jnp.dot(weight[0, 0, span, :], source, preferred_element_type=F32)
            target[span, :] = silu(out).astype(BF16)
            start += size

    def chunk(i, carry):
        first, second = 2 * i, 2 * i + 1
        states = jnp.concatenate([blocks_ref[pick[first]], blocks_ref[pick[second]]], axis=1)
        layer(first_weight, states, hidden_one, 320)
        layer(w_mid, hidden_one[...], hidden_two, 160)
        layer(w_low, hidden_two[...], hidden_three, 80)
        rates = jnp.dot(w_out[0, 0], hidden_three[...], preferred_element_type=F32)
        slots_ref[place[first]] = rates[:, :count]
        slots_ref[place[second]] = rates[:, count:]
        return carry

    lax.fori_loop(0, (found + 1) // 2, chunk, 0)


def flow_base(
    start_ref, section_ref, velocity_ref, spread_ref, halo_x_ref, halo_y_ref, base_ref
):
    fields, rows_x, rows_y = section_ref.shape
    lanes = lax.broadcasted_iota(jnp.int32, (rows_x, rows_y), 1)
    subs = lax.broadcasted_iota(jnp.int32, (rows_x, rows_y), 0)
    half_u = 0.5 * velocity_ref[0]
    half_v = 0.5 * velocity_ref[1]
    low_x = halo_x_ref[0].astype(F32)
    high_x = halo_x_ref[1].astype(F32)
    low_y = halo_y_ref[0].astype(F32)
    high_y = halo_y_ref[1].astype(F32)
    for f in range(fields):
        here = section_ref[f]
        plus_x = jnp.where(
            subs == rows_x - 1, high_x[f : f + 1], pltpu.roll(here, rows_x - 1, 0)
        )
        minus_x = jnp.where(subs == 0, low_x[f : f + 1], pltpu.roll(here, 1, 0))
        plus_y = jnp.where(
            lanes == rows_y - 1,
            pltpu.roll(high_y, rows_y - 1 - f, 1),
            pltpu.roll(here, rows_y - 1, 1),
        )
        edge = pltpu.roll(low_y, (rows_y - f) % rows_y, 1) if f else low_y
        minus_y = jnp.where(lanes == 0, edge, pltpu.roll(here, 1, 1))
        flow = (
            spread_ref[f] * (plus_x + minus_x + plus_y + minus_y - 4.0 * here)
            - half_u * (plus_x - minus_x)
            - half_v * (plus_y - minus_y)
        )
        base_ref[f] = 0.75 * start_ref[f] + 0.25 * (here + TIME_STEP * flow)


def return_kernel(
    teams,
    members,
    team_of,
    spread_ref,
    slots_ref,
    start_ref,
    section_ref,
    velocity_ref,
    halo_x_ref,
    halo_y_ref,
    own_ref,
    base_ref,
    back,
    chosen,
    got,
    send_t,
    recv_t,
    send_m,
    recv_m,
):
    team = lax.axis_index("team")
    member = lax.axis_index("member")
    barrier = greet(team, member, teams, members)
    pl.semaphore_wait(barrier, teams + members - 2)
    copies = []
    for d in spread_order(teams):
        target = lax.rem(team + d, teams)
        copy = pltpu.make_async_remote_copy(
            src_ref=slots_ref.at[pl.ds(target * CAP, CAP)],
            dst_ref=back.at[pl.ds(team * CAP, CAP)],
            send_sem=send_t.at[d],
            recv_sem=recv_t.at[d],
            device_id=(target, member),
            device_id_type=MESH,
        )
        copy.start()
        copies.append(copy)
    back[pl.ds(team * CAP, CAP)] = slots_ref[pl.ds(team * CAP, CAP)]
    assigned = [team_of[team * members + q] for q in range(members)]
    where = []
    for q in range(members):
        rank = jnp.int32(0)
        for other in range(q):
            rank = rank + (assigned[other] == assigned[q]).astype(jnp.int32)
        where.append(assigned[q] * CAP + rank)
    flow_base(
        start_ref, section_ref, velocity_ref, spread_ref, halo_x_ref, halo_y_ref, base_ref
    )
    for copy in copies:
        copy.wait_recv()
    for q in range(members):
        chosen[q] = back[where[q]]
    sends = []
    for e in range(1, members):
        target = lax.rem(member + e, members)
        copy = pltpu.make_async_remote_copy(
            src_ref=chosen.at[target],
            dst_ref=got.at[e],
            send_sem=send_m.at[e],
            recv_sem=recv_m.at[e],
            device_id=(team, target),
            device_id_type=MESH,
        )
        copy.start()
        sends.append(copy)
    total = chosen[member]
    for e, copy in enumerate(sends):
        copy.wait_recv()
        total = total + got[e + 1]
    own_ref[...] = total
    for copy in copies + sends:
        copy.wait_send()


def update_kernel(cells_ref, rates_ref, base_ref, source_ref, new_ref):
    fields, rows_x, rows_y = base_ref.shape
    cells_x, cells_y = split_cells(cells_ref[...], rows_y)
    count = cells_x.shape[1]
    pick_x = row_mask(cells_x, rows_x)
    pick_y = (lax.broadcasted_iota(jnp.int32, (rows_y, count), 0) == cells_y).astype(F32)
    pick_y = pick_y.astype(BF16)
    pick_y = jnp.concatenate([pick_y, pick_y], axis=1)
    for f in range(fields):
        spread_rates = jnp.where(pick_x, rates_ref[f : f + 1, :], 0.0)
        top = spread_rates.astype(BF16)
        rest = (spread_rates - top.astype(F32)).astype(BF16)
        source = lax.dot_general(
            jnp.concatenate([top, rest], axis=1),
            pick_y,
            (((1,), (1,)), ((), ())),
            preferred_element_type=F32,
        )
        source_ref[f] = source
        new_ref[f] = base_ref[f] + (0.25 * TIME_STEP) * source


def whole(space=VMEM):
    return pl.BlockSpec(memory_space=space)


def shards(
    state_start,
    state_section,
    velocity,
    diffusivity,
    flame_cells,
    block_team,
    w_in,
    w_mid,
    w_low,
    w_out,
):
    teams = lax.axis_size("team")
    members = lax.axis_size("member")
    fields, rows_x, rows_y = state_section.shape
    count = flame_cells.shape[1]
    team_of = block_team.reshape(-1)
    dma = pltpu.SemaphoreType.DMA
    blocks, halo_x, halo_y = pl.pallas_call(
        functools.partial(share_kernel, teams, members),
        out_shape=(
            jax.ShapeDtypeStruct((members, teams, fields, count), BF16),
            jax.ShapeDtypeStruct((2, fields, rows_y), BF16),
            jax.ShapeDtypeStruct((2, rows_x, rows_y), BF16),
        ),
        in_specs=[whole(), whole()],
        out_specs=(whole(), whole(), whole()),
        scratch_shapes=[
            VMEM((2, fields, rows_y), BF16),
            VMEM((2, rows_x, rows_y), BF16),
            dma((teams,)),
            dma((teams,)),
            dma((teams, members)),
            dma((teams, members)),
            dma((4,)),
            dma((4,)),
        ],
        compiler_params=pltpu.CompilerParams(
            collective_id=0, has_side_effects=True, vmem_limit_bytes=GRANT
        ),
        name="share",
    )(state_section, flame_cells)
    slots = pl.pallas_call(
        functools.partial(network_kernel, teams, members),
        out_shape=jax.ShapeDtypeStruct((teams * CAP, fields, count), F32),
        in_specs=[whole(pltpu.SMEM)] + [whole()] * 5,
        out_specs=whole(),
        scratch_shapes=[
            VMEM(w_in.shape, BF16),
            VMEM((w_in.shape[2], 2 * count), BF16),
            VMEM((w_mid.shape[2], 2 * count), BF16),
            VMEM((w_low.shape[2], 2 * count), BF16),
            pltpu.SMEM((teams * CAP + 2,), jnp.int32),
            pltpu.SMEM((teams * CAP + 2,), jnp.int32),
        ],
        compiler_params=pltpu.CompilerParams(vmem_limit_bytes=GRANT),
        name="networks",
    )(team_of, blocks.reshape(members * teams, fields, count), jnp.swapaxes(w_in, 2, 3), w_mid, w_low, w_out)
    rates, base = pl.pallas_call(
        functools.partial(return_kernel, teams, members),
        out_shape=(
            jax.ShapeDtypeStruct((fields, count), F32),
            jax.ShapeDtypeStruct(state_section.shape, F32),
        ),
        in_specs=[whole(pltpu.SMEM)] * 2 + [whole()] * 6,
        out_specs=(whole(), whole()),
        scratch_shapes=[
            VMEM((teams * CAP, fields, count), F32),
            VMEM((members, fields, count), F32),
            VMEM((members, fields, count), F32),
            dma((teams,)),
            dma((teams,)),
            dma((members,)),
            dma((members,)),
        ],
        compiler_params=pltpu.CompilerParams(
            collective_id=1, has_side_effects=True, vmem_limit_bytes=GRANT
        ),
        name="giveback",
    )(team_of, diffusivity, slots, state_start, state_section, velocity, halo_x, halo_y)
    step = 8 if fields % 8 == 0 else fields
    tile = pl.BlockSpec((step, rows_x, rows_y), lambda i: (i, 0, 0))
    return pl.pallas_call(
        update_kernel,
        grid=(fields // step,),
        out_shape=(
            jax.ShapeDtypeStruct(state_section.shape, F32),
            jax.ShapeDtypeStruct(state_section.shape, F32),
        ),
        in_specs=[
            pl.BlockSpec(flame_cells.shape, lambda i: (0, 0)),
            pl.BlockSpec((step, count), lambda i: (i, 0)),
            tile,
        ],
        out_specs=(tile, tile),
        compiler_params=pltpu.CompilerParams(vmem_limit_bytes=GRANT),
        name="update",
    )(flame_cells, rates, base)


def solution(mesh):
    grid = P(None, "team", "member")
    weights = P("team", "member", None, None)
    placed = (
        grid,
        grid,
        grid,
        P(),
        P(("team", "member"), None),
        P(),
        weights,
        weights,
        weights,
        weights,
    )
    return jax.shard_map(
        shards, mesh=mesh, in_specs=placed, out_specs=(grid, grid), check_vma=False
    )
```

profile of v0, /device:TPU:0, one launch (start us, length us, event | category | flops | bytes accessed | tf_op | source)
XLA Modules:
  0.0 45.2 jit_solution(15117760330272886201)
XLA Ops:
  0.6 0.0 copy-start.11
  0.6 0.0 copy-start
  0.6 1.1 %copy-done = f32[24,64,128]{2,1,0:T(8,128)S(1)} copy-done((f32[24,64,128]{2,1,0:T(8,128)S(1)}, f32[24,64,128]{2,1,0:T(8,128)}, u32[]{:S(2)}) %copy-start) | copy-done | bytes 786456
  1.8 0.0 copy-start.8
  1.8 0.7 %copy-done.8 = s32[1,128]{1,0:T(1,128)S(1)} copy-done((s32[1,128]{1,0:T(1,128)S(1)}, s32[1,128]{1,0:T(1,128)}, u32[]{:S(2)}) %copy-start.8) | copy-done | bytes 536
  2.4 0.0 copy-start.1
  2.4 13.0 %share.1 = (bf16[4,8,24,128]{3,2,1,0:T(8,128)(2,1)S(1)}, bf16[2,24,128]{2,1,0:T(8,128)(2,1)S(1)}, bf16[2,64,128]{2,1,0:T(8,128)(2,1)S(1)}) custom-call(f32[24,64,128]{2,1,0:T(8,128)S(1)} %copy-done, s32[1,128]{1,0:T(1,128)S(1)} %copy-done.8), custom_call_target="tpu_custom_call" | custom-call | tf_op jit(solution)/shard_map/share/pallas_call | solution.py:375
  15.4 0.0 copy-start.2
  15.5 1.7 %copy-done.2 = bf16[1,1,800,1600]{3,2,1,0:T(8,128)(2,1)S(1)} copy-done((bf16[1,1,800,1600]{3,2,1,0:T(8,128)(2,1)S(1)}, bf16[1,1,800,1600]{3,2,1,0:T(8,128)(2,1)}, u32[]{:S(2)}) %copy-start.2) | copy-done | bytes 2560024
  17.2 0.0 copy-start.4
  17.2 1.1 %copy-done.4 = bf16[1,1,400,800]{3,2,1,0:T(8,128)(2,1)S(1)} copy-done((bf16[1,1,400,800]{3,2,1,0:T(8,128)(2,1)S(1)}, bf16[1,1,400,800]{3,2,1,0:T(8,128)(2,1)}, u32[]{:S(2)}) %copy-start.4) | copy-done | bytes 640024
  18.3 0.0 copy-start.5
  18.3 0.9 %copy-done.5 = bf16[1,1,1600,24]{2,3,1,0:T(8,128)(2,1)S(1)} copy-done((bf16[1,1,1600,24]{2,3,1,0:T(8,128)(2,1)S(1)}, bf16[1,1,1600,24]{2,3,1,0:T(8,128)(2,1)}, u32[]{:S(2)}) %copy-start.5) | copy-done | bytes 76824
  19.2 0.0 copy-start.7
  19.2 0.7 %copy-done.7 = bf16[1,1,24,400]{3,2,1,0:T(8,128)(2,1)S(1)} copy-done((bf16[1,1,24,400]{3,2,1,0:T(8,128)(2,1)S(1)}, bf16[1,1,24,400]{3,2,1,0:T(8,128)(2,1)}, u32[]{:S(2)}) %copy-start.7) | copy-done | bytes 19224
  19.9 0.0 copy-start.10
  19.9 0.7 %copy-done.10 = s32[32,1]{0,1:T(1,128)S(1)} copy-done((s32[32,1]{0,1:T(1,128)S(1)}, s32[32,1]{0,1:T(1,128)}, u32[]{:S(2)}) %copy-start.10) | copy-done | bytes 152
  20.6 0.0 copy-start.3
  20.6 0.0 copy-start.6
  20.6 0.0 copy-start.9
  20.6 2.8 %networks.1.slots_ref = f32[16,24,128]{2,1,0:T(8,128)S(1)} custom-call(s32[32]{0:T(128)S(1)} %bitcast.5, bf16[32,24,128]{2,1,0:T(8,128)(2,1)S(1)} %bitcast.3, bf16[1,1,24,1600]{3,2,1,0:T(8,128)(2,1)S(1)} %bitcast.4, bf16[1,1,800,1600]{3,2,1,0:T(8,128)(2,1)S(1)} %copy-done.2, bf16[1,1,400,800]{3,2,1,0:T(8,128)(2,1)S(1)} %copy-done.4, ...), custom_call_target="tpu_custom_call" | custom-call | tf_op jit(solution)/shard_map/networks/pallas_call | solution.py:399
  23.4 0.0 copy-done.11
  23.4 0.0 copy-done.1
  23.4 0.0 copy-done.3
  23.4 0.0 copy-done.6
  23.4 19.5 %giveback.1 = (f32[24,128]{1,0:T(8,128)S(1)}, f32[24,64,128]{2,1,0:T(8,128)S(1)}) custom-call(s32[32]{0:T(128)S(1)} %bitcast.6, f32[24]{0:T(128)S(1)} %copy-done.11, f32[16,24,128]{2,1,0:T(8,128)S(1)} %networks.1.slots_ref, f32[24,64,128]{2,1,0:T(8,128)S(1)} %copy-done.3, f32[24,64,128]{2,1,0:T(8,128)S(1)} %copy-done.1, f32[2,64,128]{2,1,0:T(8,128)S(1)} %copy-done.6, ...), custom_call_target="tpu_custom_call" | custom-call | tf_op jit(solution)/shard_map/giveback/pallas_call | solution.py:415
  43.0 0.0 copy-done.9
  43.0 2.2 %update.1 = (f32[24,64,128]{2,1,0:T(8,128)}, f32[24,64,128]{2,1,0:T(8,128)}) custom-call(s32[1,128]{1,0:T(1,128)S(1)} %copy-done.9, f32[24,128]{1,0:T(8,128)S(1)} %get-tuple-element.10.rates_ref, f32[24,64,128]{2,1,0:T(8,128)S(1)} %get-tuple-element.11.base_ref), custom_call_target="tpu_custom_call" | custom-call | tf_op jit(solution)/shard_map/update/pallas_call | solution.py:439
Async XLA Ops:
  0.6 22.8 %copy-start.11 = (f32[24]{0:T(128)S(1)}, f32[24]{0:T(128)}, u32[]{:S(2)}) copy-start(f32[24]{0:T(128)} %spread_ref.1) | copy-start | bytes 292
  0.6 1.1 %copy-start = (f32[24,64,128]{2,1,0:T(8,128)S(1)}, f32[24,64,128]{2,1,0:T(8,128)}, u32[]{:S(2)}) copy-start(f32[24,64,128]{2,1,0:T(8,128)} %section_ref.3) | copy-start | bytes 2359300
  1.8 0.7 %copy-start.8 = (s32[1,128]{1,0:T(1,128)S(1)}, s32[1,128]{1,0:T(1,128)}, u32[]{:S(2)}) copy-start(s32[1,128]{1,0:T(1,128)} %cells_ref.3) | copy-start | bytes 1540
  2.4 21.0 %copy-start.1 = (f32[24,64,128]{2,1,0:T(8,128)S(1)}, f32[24,64,128]{2,1,0:T(8,128)}, u32[]{:S(2)}) copy-start(f32[24,64,128]{2,1,0:T(8,128)} %section_ref.3) | copy-start | bytes 2359300
  15.4 1.8 %copy-start.2 = (bf16[1,1,800,1600]{3,2,1,0:T(8,128)(2,1)S(1)}, bf16[1,1,800,1600]{3,2,1,0:T(8,128)(2,1)}, u32[]{:S(2)}) copy-start(bf16[1,1,800,1600]{3,2,1,0:T(8,128)(2,1)} %w_mid.1) | copy-start | bytes 7680004
  17.2 1.1 %copy-start.4 = (bf16[1,1,400,800]{3,2,1,0:T(8,128)(2,1)S(1)}, bf16[1,1,400,800]{3,2,1,0:T(8,128)(2,1)}, u32[]{:S(2)}) copy-start(bf16[1,1,400,800]{3,2,1,0:T(8,128)(2,1)} %w_low.1) | copy-start | bytes 1920004
  18.3 0.9 %copy-start.5 = (bf16[1,1,1600,24]{2,3,1,0:T(8,128)(2,1)S(1)}, bf16[1,1,1600,24]{2,3,1,0:T(8,128)(2,1)}, u32[]{:S(2)}) copy-start(bf16[1,1,1600,24]{2,3,1,0:T(8,128)(2,1)} %param.16) | copy-start | bytes 230404
  19.2 0.7 %copy-start.7 = (bf16[1,1,24,400]{3,2,1,0:T(8,128)(2,1)S(1)}, bf16[1,1,24,400]{3,2,1,0:T(8,128)(2,1)}, u32[]{:S(2)}) copy-start(bf16[1,1,24,400]{3,2,1,0:T(8,128)(2,1)} %w_out.1) | copy-start | bytes 57604
  19.9 0.7 %copy-start.10 = (s32[32,1]{0,1:T(1,128)S(1)}, s32[32,1]{0,1:T(1,128)}, u32[]{:S(2)}) copy-start(s32[32,1]{0,1:T(1,128)} %param.15) | copy-start | bytes 388
  20.6 2.8 %copy-start.3 = (f32[24,64,128]{2,1,0:T(8,128)S(1)}, f32[24,64,128]{2,1,0:T(8,128)}, u32[]{:S(2)}) copy-start(f32[24,64,128]{2,1,0:T(8,128)} %start_ref.1) | copy-start | bytes 2359300
  20.6 2.8 %copy-start.6 = (f32[2,64,128]{2,1,0:T(8,128)S(1)}, f32[2,64,128]{2,1,0:T(8,128)}, u32[]{:S(2)}) copy-start(f32[2,64,128]{2,1,0:T(8,128)} %velocity_ref.1) | copy-start | bytes 196612
  20.6 22.4 %copy-start.9 = (s32[1,128]{1,0:T(1,128)S(1)}, s32[1,128]{1,0:T(1,128)}, u32[]{:S(2)}) copy-start(s32[1,128]{1,0:T(1,128)} %cells_ref.3) | copy-start | bytes 1540
where the time goes:
time: 45.1 us; the launch traced here: 45.2 us
  Pallas kernels  37.5 us (83%)
  local copies, waits for them, and re-layouts  6.95 us (15%)
  between operations  0.71 us (2%)
    pallas_call x1, Pallas kernels, shards(): pl.pallas_call(functools.partial(return_kernel, teams, members), out_shap...  19.5 us
    pallas_call x1, Pallas kernels, shards(): pl.pallas_call(functools.partial(share_kernel, teams, members), out_shape...  13 us
    unnamed x24, local copies, waits for them, and re-layouts  6.95 us
    pallas_call x1, Pallas kernels, shards(): pl.pallas_call(functools.partial(network_kernel, teams, members), out_sha...  2.78 us
    pallas_call x1, Pallas kernels, shards(): pl.pallas_call(update_kernel, grid=(fields // step,), out_shape=(jax.Shap...  2.23 us

commit v1 on v0

--- a/solution.py
+++ b/solution.py
@@ -57,13 +57,25 @@
 def share_kernel(
     teams,
     members,
-    section_ref,
-    cells_ref,
+    section_hbm,
+    cells_hbm,
+    w_in_hbm,
+    w_mid_hbm,
+    w_low_hbm,
+    w_out_hbm,
     blocks_ref,
     halo_x_ref,
     halo_y_ref,
+    w_in_ref,
+    w_mid_ref,
+    w_low_ref,
+    w_out_ref,
+    section_ref,
+    cells_ref,
+    w_in_raw,
     edge_x,
     edge_y,
+    load_sem,
     send_t,
     recv_t,
     send_m,
@@ -74,28 +86,32 @@
     team = lax.axis_index("team")
     member = lax.axis_index("member")
     barrier = greet(team, member, teams, members)
+    loads = []
+    for k, (source, target) in enumerate(
+        (
+            (section_hbm, section_ref),
+            (cells_hbm, cells_ref),
+            (w_in_hbm, w_in_raw),
+            (w_mid_hbm, w_mid_ref),
+            (w_low_hbm, w_low_ref),
+            (w_out_hbm, w_out_ref),
+        )
+    ):
+        copy = pltpu.make_async_copy(source, target, load_sem.at[k])
+        copy.start()
+        loads.append(copy)
+    loads[1].wait()
     fields, rows_x, rows_y = section_ref.shape
     cells_x, cells_y = split_cells(cells_ref[...], rows_y)
     count = cells_x.shape[1]
     pick_y = (lax.broadcasted_iota(jnp.int32, (rows_y, count), 0) == cells_y).astype(F32)
     pick_x = row_mask(cells_x, rows_x)
+    loads[0].wait()
     flat = section_ref[...].reshape(fields * rows_x, rows_y).astype(BF16)
     taken = jnp.dot(flat, pick_y.astype(BF16), preferred_element_type=F32)
     taken = taken.reshape(fields, rows_x, count)
     own = jnp.sum(jnp.where(pick_x[None], taken, 0.0), axis=1)
     blocks_ref[member, team] = own.astype(BF16)
-    edge_x[0] = section_ref[:, rows_x - 1, :].astype(BF16)
-    edge_x[1] = section_ref[:, 0, :].astype(BF16)
-    lanes = lax.broadcasted_iota(jnp.int32, (rows_x, rows_y), 1)
-    low = jnp.zeros((rows_x, rows_y), F32)
-    high = jnp.zeros((rows_x, rows_y), F32)
-    for f in range(fields):
-        plane = section_ref[f]
-        here = lanes == f
-        high = jnp.where(here, pltpu.roll(plane, (f + 1) % rows_y, 1), high)
-        low = jnp.where(here, pltpu.roll(plane, f, 1) if f else plane, low)
-    edge_y[0] = high.astype(BF16)
-    edge_y[1] = low.astype(BF16)
     pl.semaphore_wait(barrier, teams + members - 2)
 
     started = []
@@ -127,6 +143,18 @@
             started.append(copy)
 
     forward(0)
+    edge_x[0] = section_ref[:, rows_x - 1, :].astype(BF16)
+    edge_x[1] = section_ref[:, 0, :].astype(BF16)
+    lanes = lax.broadcasted_iota(jnp.int32, (rows_x, rows_y), 1)
+    low = jnp.zeros((rows_x, rows_y), F32)
+    high = jnp.zeros((rows_x, rows_y), F32)
+    for f in range(fields):
+        plane = section_ref[f]
+        here = lanes == f
+        high = jnp.where(here, pltpu.roll(plane, (f + 1) % rows_y, 1), high)
+        low = jnp.where(here, pltpu.roll(plane, f, 1) if f else plane, low)
+    edge_y[0] = high.astype(BF16)
+    edge_y[1] = low.astype(BF16)
     halos = []
     for k, (step, edge, halo, along) in enumerate(
         (
@@ -150,10 +178,12 @@
         )
         copy.start()
         halos.append(copy)
+    loads[2].wait()
+    w_in_ref[0, 0] = w_in_raw[0, 0].T
     for d in spread_order(teams):
         t_copies[d].wait_recv()
         forward(d)
-    for copy in started + halos:
+    for copy in started + halos + loads[3:]:
         copy.wait()
     for d in spread_order(teams):
         t_copies[d].wait_send()
@@ -169,7 +199,6 @@
     w_low,
     w_out,
     slots_ref,
-    first_weight,
     hidden_one,
     hidden_two,
     hidden_three,
@@ -190,7 +219,6 @@
             seen = seen + mine
         return found
 
-    first_weight[0, 0] = w_in[0, 0].T
     found = lax.fori_loop(0, teams, scan_team, jnp.int32(0))
     last = jnp.maximum(found - 1, 0)
     pick[found] = pick[last]
@@ -209,7 +237,7 @@
     def chunk(i, carry):
         first, second = 2 * i, 2 * i + 1
         states = jnp.concatenate([blocks_ref[pick[first]], blocks_ref[pick[second]]], axis=1)
-        layer(first_weight, states, hidden_one, 320)
+        layer(w_in, states, hidden_one, 320)
         layer(w_mid, hidden_one[...], hidden_two, 160)
         layer(w_low, hidden_two[...], hidden_three, 80)
         rates = jnp.dot(w_out[0, 0], hidden_three[...], preferred_element_type=F32)
@@ -372,18 +400,28 @@
     count = flame_cells.shape[1]
     team_of = block_team.reshape(-1)
     dma = pltpu.SemaphoreType.DMA
-    blocks, halo_x, halo_y = pl.pallas_call(
+    w_in = jnp.swapaxes(w_in, 2, 3)
+    hidden = w_in.shape[3]
+    blocks, halo_x, halo_y, w_in, w_mid, w_low, w_out = pl.pallas_call(
         functools.partial(share_kernel, teams, members),
         out_shape=(
             jax.ShapeDtypeStruct((members, teams, fields, count), BF16),
             jax.ShapeDtypeStruct((2, fields, rows_y), BF16),
             jax.ShapeDtypeStruct((2, rows_x, rows_y), BF16),
+            jax.ShapeDtypeStruct((1, 1, hidden, fields), BF16),
+            jax.ShapeDtypeStruct(w_mid.shape, BF16),
+            jax.ShapeDtypeStruct(w_low.shape, BF16),
+            jax.ShapeDtypeStruct(w_out.shape, BF16),
         ),
-        in_specs=[whole(), whole()],
-        out_specs=(whole(), whole(), whole()),
+        in_specs=[whole(pltpu.HBM)] * 6,
+        out_specs=(whole(),) * 7,
         scratch_shapes=[
+            VMEM(state_section.shape, F32),
+            VMEM(flame_cells.shape, jnp.int32),
+            VMEM(w_in.shape, BF16),
             VMEM((2, fields, rows_y), BF16),
             VMEM((2, rows_x, rows_y), BF16),
+            dma((6,)),
             dma((teams,)),
             dma((teams,)),
             dma((teams, members)),
@@ -395,14 +433,13 @@
             collective_id=0, has_side_effects=True, vmem_limit_bytes=GRANT
         ),
         name="share",
-    )(state_section, flame_cells)
+    )(state_section, flame_cells, w_in, w_mid, w_low, w_out)
     slots = pl.pallas_call(
         functools.partial(network_kernel, teams, members),
         out_shape=jax.ShapeDtypeStruct((teams * CAP, fields, count), F32),
         in_specs=[whole(pltpu.SMEM)] + [whole()] * 5,
         out_specs=whole(),
         scratch_shapes=[
-            VMEM(w_in.shape, BF16),
             VMEM((w_in.shape[2], 2 * count), BF16),
             VMEM((w_mid.shape[2], 2 * count), BF16),
             VMEM((w_low.shape[2], 2 * count), BF16),
@@ -411,7 +448,7 @@
         ],
         compiler_params=pltpu.CompilerParams(vmem_limit_bytes=GRANT),
         name="networks",
-    )(team_of, blocks.reshape(members * teams, fields, count), jnp.swapaxes(w_in, 2, 3), w_mid, w_low, w_out)
+    )(team_of, blocks.reshape(members * teams, fields, count), w_in, w_mid, w_low, w_out)
     rates, base = pl.pallas_call(
         functools.partial(return_kernel, teams, members),
         out_shape=(

time: 45.1 us -> 43.6 us (0.967)
  Pallas kernels: 37.5 us -> 36.3 us
  local copies, waits for them, and re-layouts: 6.95 us -> 6.31 us
    pallas_call x1, Pallas kernels: 19.5 us -> 18.2 us  [shards(): pl.pallas_call(functools.partial(return_kernel, teams, members), out_shap...]
    unnamed x24 -> x22, local copies, waits for them, and re-layouts: 6.95 us -> 6.31 us
where the time goes in v1:
time: 43.6 us; the launch traced here: 43.3 us
  Pallas kernels  36.3 us (83%)
  local copies, waits for them, and re-layouts  6.31 us (14%)
  between operations  0.73 us (2%)
    pallas_call x1, Pallas kernels, shards(): pl.pallas_call(functools.partial(return_kernel, teams, members), out_shap...  18.2 us
    pallas_call x1, Pallas kernels, shards(): pl.pallas_call(functools.partial(share_kernel, teams, members), out_shape...  13.2 us
    unnamed x22, local copies, waits for them, and re-layouts  6.31 us
    pallas_call x1, Pallas kernels, shards(): pl.pallas_call(functools.partial(network_kernel, teams, members), out_sha...  2.63 us
    pallas_call x1, Pallas kernels, shards(): pl.pallas_call(update_kernel, grid=(fields // step,), out_shape=(jax.Shap...  2.23 us

profile of v1, /device:TPU:0, one launch (start us, length us, event | category | flops | bytes accessed | tf_op | source)
XLA Modules:
  0.0 43.3 jit_solution(12296788601614342952)
XLA Ops:
  0.6 0.0 copy-start.8
  0.6 0.0 copy-start
  0.7 1.1 %copy-done = f32[24,64,128]{2,1,0:T(8,128)S(1)} copy-done((f32[24,64,128]{2,1,0:T(8,128)S(1)}, f32[24,64,128]{2,1,0:T(8,128)}, u32[]{:S(2)}) %copy-start) | copy-done | bytes 786456
  1.8 0.0 copy-start.2
  1.8 1.7 %copy-done.2 = bf16[1,1,800,1600]{3,2,1,0:T(8,128)(2,1)S(1)} copy-done((bf16[1,1,800,1600]{3,2,1,0:T(8,128)(2,1)S(1)}, bf16[1,1,800,1600]{3,2,1,0:T(8,128)(2,1)}, u32[]{:S(2)}) %copy-start.2) | copy-done | bytes 2560024
  3.5 0.0 copy-start.4
  3.5 1.1 %copy-done.4 = bf16[1,1,400,800]{3,2,1,0:T(8,128)(2,1)S(1)} copy-done((bf16[1,1,400,800]{3,2,1,0:T(8,128)(2,1)S(1)}, bf16[1,1,400,800]{3,2,1,0:T(8,128)(2,1)}, u32[]{:S(2)}) %copy-start.4) | copy-done | bytes 640024
  4.6 0.0 copy-start.5
  4.6 0.9 %copy-done.5 = bf16[1,1,1600,24]{2,3,1,0:T(8,128)(2,1)S(1)} copy-done((bf16[1,1,1600,24]{2,3,1,0:T(8,128)(2,1)S(1)}, bf16[1,1,1600,24]{2,3,1,0:T(8,128)(2,1)}, u32[]{:S(2)}) %copy-start.5) | copy-done | bytes 76824
  5.5 0.0 copy-start.7
  5.5 0.7 %copy-done.7 = bf16[1,1,24,400]{3,2,1,0:T(8,128)(2,1)S(1)} copy-done((bf16[1,1,24,400]{3,2,1,0:T(8,128)(2,1)S(1)}, bf16[1,1,24,400]{3,2,1,0:T(8,128)(2,1)}, u32[]{:S(2)}) %copy-start.7) | copy-done | bytes 19224
  6.3 0.0 copy-start.9
  6.3 0.7 %copy-done.9 = s32[1,128]{1,0:T(1,128)S(1)} copy-done((s32[1,128]{1,0:T(1,128)S(1)}, s32[1,128]{1,0:T(1,128)}, u32[]{:S(2)}) %copy-start.9) | copy-done | bytes 536
  6.9 13.2 %share.1 = (bf16[4,8,24,128]{3,2,1,0:T(8,128)(2,1)S(1)}, bf16[2,24,128]{2,1,0:T(8,128)(2,1)S(1)}, bf16[2,64,128]{2,1,0:T(8,128)(2,1)S(1)}, bf16[1,1,1600,24]{3,2...) custom-call(f32[24,64,128]{2,1,0:T(8,128)S(1)} %copy-done, ...), custom_call_target="tpu_custom_call" | custom-call | tf_op jit(solution)/shard_map/share/pallas_call | solution.py:405
  20.1 0.0 copy-start.1
  20.1 0.0 copy-start.3
  20.2 0.0 copy-start.6
  20.2 0.0 copy-start.10
  20.2 0.0 copy-done.8
  20.2 2.6 %networks.1.slots_ref = f32[16,24,128]{2,1,0:T(8,128)S(1)} custom-call(s32[32]{0:T(128)S(1)} %bitcast.5, bf16[32,24,128]{2,1,0:T(8,128)(2,1)S(1)} %bitcast.3, bf16[1,1,1600,24]{3,2,1,0:T(8,128)(2,1)S(1)} %get-tuple-element.12.w_in, bf16[1,1,800,1600]{3,2,1,0:T(8,128)(2,1)S(1)} %get-tuple-element.13.w_mid, ...), custom_call_target="tpu_custom_call" | custom-call | tf_op jit(solution)/shard_map/networks/pallas_call | solution.py:437
  22.8 0.0 copy-done.1
  22.8 0.0 copy-done.3
  22.8 0.0 copy-done.6
  22.8 0.0 copy-done.10
  22.9 18.2 %giveback.1 = (f32[24,128]{1,0:T(8,128)S(1)}, f32[24,64,128]{2,1,0:T(8,128)S(1)}) custom-call(s32[32]{0:T(128)S(1)} %bitcast.6, f32[24]{0:T(128)S(1)} %copy-done.10, f32[16,24,128]{2,1,0:T(8,128)S(1)} %networks.1.slots_ref, f32[24,64,128]{2,1,0:T(8,128)S(1)} %copy-done.3, f32[24,64,128]{2,1,0:T(8,128)S(1)} %copy-done.1, f32[2,64,128]{2,1,0:T(8,128)S(1)} %copy-done.6, ...), custom_call_target="tpu_custom_call" | custom-call | tf_op jit(solution)/shard_map/giveback/pallas_call | solution.py:452
  41.1 2.2 %update.1 = (f32[24,64,128]{2,1,0:T(8,128)}, f32[24,64,128]{2,1,0:T(8,128)}) custom-call(s32[1,128]{1,0:T(1,128)S(1)} %copy-done.9, f32[24,128]{1,0:T(8,128)S(1)} %get-tuple-element.18.rates_ref, f32[24,64,128]{2,1,0:T(8,128)S(1)} %get-tuple-element.19.base_ref), custom_call_target="tpu_custom_call" | custom-call | tf_op jit(solution)/shard_map/update/pallas_call | solution.py:476
Async XLA Ops:
  0.6 19.5 %copy-start.8 = (s32[32,1]{0,1:T(1,128)S(1)}, s32[32,1]{0,1:T(1,128)}, u32[]{:S(2)}) copy-start(s32[32,1]{0,1:T(1,128)} %param.15) | copy-start | bytes 388
  0.6 1.1 %copy-start = (f32[24,64,128]{2,1,0:T(8,128)S(1)}, f32[24,64,128]{2,1,0:T(8,128)}, u32[]{:S(2)}) copy-start(f32[24,64,128]{2,1,0:T(8,128)} %section_ref.1) | copy-start | bytes 2359300
  1.8 1.8 %copy-start.2 = (bf16[1,1,800,1600]{3,2,1,0:T(8,128)(2,1)S(1)}, bf16[1,1,800,1600]{3,2,1,0:T(8,128)(2,1)}, u32[]{:S(2)}) copy-start(bf16[1,1,800,1600]{3,2,1,0:T(8,128)(2,1)} %w_mid_hbm.1) | copy-start | bytes 7680004
  3.5 1.1 %copy-start.4 = (bf16[1,1,400,800]{3,2,1,0:T(8,128)(2,1)S(1)}, bf16[1,1,400,800]{3,2,1,0:T(8,128)(2,1)}, u32[]{:S(2)}) copy-start(bf16[1,1,400,800]{3,2,1,0:T(8,128)(2,1)} %w_low_hbm.1) | copy-start | bytes 1920004
  4.6 0.9 %copy-start.5 = (bf16[1,1,1600,24]{2,3,1,0:T(8,128)(2,1)S(1)}, bf16[1,1,1600,24]{2,3,1,0:T(8,128)(2,1)}, u32[]{:S(2)}) copy-start(bf16[1,1,1600,24]{2,3,1,0:T(8,128)(2,1)} %param.16) | copy-start | bytes 230404
  5.5 0.7 %copy-start.7 = (bf16[1,1,24,400]{3,2,1,0:T(8,128)(2,1)S(1)}, bf16[1,1,24,400]{3,2,1,0:T(8,128)(2,1)}, u32[]{:S(2)}) copy-start(bf16[1,1,24,400]{3,2,1,0:T(8,128)(2,1)} %w_out_hbm.1) | copy-start | bytes 57604
  6.3 0.7 %copy-start.9 = (s32[1,128]{1,0:T(1,128)S(1)}, s32[1,128]{1,0:T(1,128)}, u32[]{:S(2)}) copy-start(s32[1,128]{1,0:T(1,128)} %cells_ref.1) | copy-start | bytes 1540
  20.1 2.7 %copy-start.1 = (f32[24,64,128]{2,1,0:T(8,128)S(1)}, f32[24,64,128]{2,1,0:T(8,128)}, u32[]{:S(2)}) copy-start(f32[24,64,128]{2,1,0:T(8,128)} %section_ref.1) | copy-start | bytes 2359300
  20.1 2.7 %copy-start.3 = (f32[24,64,128]{2,1,0:T(8,128)S(1)}, f32[24,64,128]{2,1,0:T(8,128)}, u32[]{:S(2)}) copy-start(f32[24,64,128]{2,1,0:T(8,128)} %start_ref.1) | copy-start | bytes 2359300
  20.2 2.7 %copy-start.6 = (f32[2,64,128]{2,1,0:T(8,128)S(1)}, f32[2,64,128]{2,1,0:T(8,128)}, u32[]{:S(2)}) copy-start(f32[2,64,128]{2,1,0:T(8,128)} %velocity_ref.1) | copy-start | bytes 196612
  20.2 2.7 %copy-start.10 = (f32[24]{0:T(128)S(1)}, f32[24]{0:T(128)}, u32[]{:S(2)}) copy-start(f32[24]{0:T(128)} %spread_ref.1) | copy-start | bytes 292

commit v2 on v1

--- a/solution.py
+++ b/solution.py
@@ -16,13 +16,14 @@
 BF16 = jnp.bfloat16
 
 
-def spread_order(count):
-    order = []
-    for step in range(1, count // 2 + 1):
-        order.append(step)
-        if count - step != step:
-            order.append(count - step)
-    return order
+def partner(index, flips):
+    target = index
+    bit = 1
+    while bit <= flips:
+        if flips & bit:
+            target = target + bit - 2 * bit * lax.rem(index // bit, 2)
+        bit *= 2
+    return target
 
 
 def split_cells(cells, rows_y):
@@ -45,11 +46,11 @@
     barrier = pltpu.get_barrier_semaphore()
     for d in range(1, teams):
         pl.semaphore_signal(
-            barrier, inc=1, device_id=(lax.rem(team + d, teams), member), device_id_type=MESH
+            barrier, inc=1, device_id=(partner(team, d), member), device_id_type=MESH
         )
     for e in range(1, members):
         pl.semaphore_signal(
-            barrier, inc=1, device_id=(team, lax.rem(member + e, members)), device_id_type=MESH
+            barrier, inc=1, device_id=(team, partner(member, e)), device_id_type=MESH
         )
     return barrier
 
@@ -116,27 +117,27 @@
 
     started = []
     t_copies = {}
-    for d in spread_order(teams):
+    for d in range(teams - 1, 0, -1):
         copy = pltpu.make_async_remote_copy(
             src_ref=blocks_ref.at[member, team],
             dst_ref=blocks_ref.at[member, team],
             send_sem=send_t.at[d],
             recv_sem=recv_t.at[d],
-            device_id=(lax.rem(team + d, teams), member),
+            device_id=(partner(team, d), member),
             device_id_type=MESH,
         )
         copy.start()
         t_copies[d] = copy
 
     def forward(d):
-        source = lax.rem(team - d + teams, teams)
-        for e in range(1, members):
+        source = partner(team, d)
+        for e in range(members - 1, 0, -1):
             copy = pltpu.make_async_remote_copy(
                 src_ref=blocks_ref.at[member, source],
                 dst_ref=blocks_ref.at[member, source],
                 send_sem=send_m.at[d, e],
                 recv_sem=recv_m.at[d, e],
-                device_id=(team, lax.rem(member + e, members)),
+                device_id=(team, partner(member, e)),
                 device_id_type=MESH,
             )
             copy.start()
@@ -180,12 +181,12 @@
         halos.append(copy)
     loads[2].wait()
     w_in_ref[0, 0] = w_in_raw[0, 0].T
-    for d in spread_order(teams):
+    for d in range(1, teams):
         t_copies[d].wait_recv()
         forward(d)
     for copy in started + halos + loads[3:]:
         copy.wait()
-    for d in spread_order(teams):
+    for d in range(1, teams):
         t_copies[d].wait_send()
 
 
@@ -307,8 +308,8 @@
     barrier = greet(team, member, teams, members)
     pl.semaphore_wait(barrier, teams + members - 2)
     copies = []
-    for d in spread_order(teams):
-        target = lax.rem(team + d, teams)
+    for d in range(teams - 1, 0, -1):
+        target = partner(team, d)
         copy = pltpu.make_async_remote_copy(
             src_ref=slots_ref.at[pl.ds(target * CAP, CAP)],
             dst_ref=back.at[pl.ds(team * CAP, CAP)],
@@ -335,8 +336,8 @@
     for q in range(members):
         chosen[q] = back[where[q]]
     sends = []
-    for e in range(1, members):
-        target = lax.rem(member + e, members)
+    for e in range(members - 1, 0, -1):
+        target = partner(member, e)
         copy = pltpu.make_async_remote_copy(
             src_ref=chosen.at[target],
             dst_ref=got.at[e],
@@ -348,9 +349,9 @@
         copy.start()
         sends.append(copy)
     total = chosen[member]
-    for e, copy in enumerate(sends):
-        copy.wait_recv()
-        total = total + got[e + 1]
+    for e in range(1, members):
+        sends[members - 1 - e].wait_recv()
+        total = total + got[e]
     own_ref[...] = total
     for copy in copies + sends:
         copy.wait_send()
@@ -433,7 +434,8 @@
             collective_id=0, has_side_effects=True, vmem_limit_bytes=GRANT
         ),
         name="share",
-    )(state_section, flame_cells, w_in, w_mid, w_low, w_out)
+    )(*[pltpu.with_memory_space_constraint(x, pltpu.HBM)
+       for x in (state_section, flame_cells, w_in, w_mid, w_low, w_out)])
     slots = pl.pallas_call(
         functools.partial(network_kernel, teams, members),
         out_shape=jax.ShapeDtypeStruct((teams * CAP, fields, count), F32),

time: 43.6 us -> 37.2 us (0.85)
  local copies, waits for them, and re-layouts: 6.31 us -> 0.04 us
  Pallas kernels: 36.3 us -> 35.7 us
    unnamed x22 -> x12, local copies, waits for them, and re-layouts: 6.31 us -> 0.04 us
    pallas_call x1, Pallas kernels: 18.2 us -> 17.6 us  [shards(): pl.pallas_call(functools.partial(return_kernel, teams, members), out_shap...]
where the time goes in v2:
time: 37.2 us; the launch traced here: 36.5 us
  Pallas kernels  35.7 us (96%)
  between operations  0.74 us (2%)
    pallas_call x1, Pallas kernels, shards(): pl.pallas_call(functools.partial(return_kernel, teams, members), out_shap...  17.6 us
    pallas_call x1, Pallas kernels, shards(): pl.pallas_call(functools.partial(share_kernel, teams, members), out_shape...  13.3 us
    pallas_call x1, Pallas kernels, shards(): pl.pallas_call(functools.partial(network_kernel, teams, members), out_sha...  2.61 us
    pallas_call x1, Pallas kernels, shards(): pl.pallas_call(update_kernel, grid=(fields // step,), out_shape=(jax.Shap...  2.22 us

profile of v2, /device:TPU:0, one launch (start us, length us, event | category | flops | bytes accessed | tf_op | source)
XLA Modules:
  0.0 36.5 jit_solution(128266690505821895)
XLA Ops:
  0.6 0.0 copy-start.3
  0.6 13.3 %share.1 = (bf16[4,8,24,128]{3,2,1,0:T(8,128)(2,1)S(1)}, bf16[2,24,128]{2,1,0:T(8,128)(2,1)S(1)}, bf16[2,64,128]{2,1,0:T(8,128)(2,1)S(1)}, bf16[1,1,1600,24]{3,2...) custom-call(f32[24,64,128]{2,1,0:T(8,128)} %section_ref.1, ...), custom_call_target="tpu_custom_call" | custom-call | tf_op jit(solution)/shard_map/share/pallas_call | solution.py:406
  14.0 0.0 copy-start
  14.0 0.0 copy-start.1
  14.0 0.0 copy-start.2
  14.0 0.0 copy-start.5
  14.0 0.0 copy-done.3
  14.0 0.0 copy-start.4
  14.1 2.6 %networks.1.slots_ref = f32[16,24,128]{2,1,0:T(8,128)S(1)} custom-call(s32[32]{0:T(128)S(1)} %bitcast.4, bf16[32,24,128]{2,1,0:T(8,128)(2,1)S(1)} %bitcast.3, bf16[1,1,1600,24]{3,2,1,0:T(8,128)(2,1)S(1)} %get-tuple-element.12.w_in, bf16[1,1,800,1600]{3,2,1,0:T(8,128)(2,1)S(1)} %get-tuple-element.13.w_mid, ...), custom_call_target="tpu_custom_call" | custom-call | tf_op jit(solution)/shard_map/networks/pallas_call | solution.py:439
  16.7 0.0 copy-done
  16.7 0.0 copy-done.1
  16.7 0.0 copy-done.2
  16.7 0.0 copy-done.5
  16.7 17.6 %giveback.1 = (f32[24,128]{1,0:T(8,128)S(1)}, f32[24,64,128]{2,1,0:T(8,128)S(1)}) custom-call(s32[32]{0:T(128)S(1)} %bitcast.5, f32[24]{0:T(128)S(1)} %copy-done.5, f32[16,24,128]{2,1,0:T(8,128)S(1)} %networks.1.slots_ref, f32[24,64,128]{2,1,0:T(8,128)S(1)} %copy-done.1, f32[24,64,128]{2,1,0:T(8,128)S(1)} %copy-done, f32[2,64,128]{2,1,0:T(8,128)S(1)} %copy-done.2, ...), custom_call_target="tpu_custom_call" | custom-call | tf_op jit(solution)/shard_map/giveback/pallas_call | solution.py:454
  34.3 0.0 copy-done.4
  34.3 2.2 %update.1 = (f32[24,64,128]{2,1,0:T(8,128)}, f32[24,64,128]{2,1,0:T(8,128)}) custom-call(s32[1,128]{1,0:T(1,128)S(1)} %copy-done.4, f32[24,128]{1,0:T(8,128)S(1)} %get-tuple-element.18.rates_ref, f32[24,64,128]{2,1,0:T(8,128)S(1)} %get-tuple-element.19.base_ref), custom_call_target="tpu_custom_call" | custom-call | tf_op jit(solution)/shard_map/update/pallas_call | solution.py:478
Async XLA Ops:
  0.6 13.4 %copy-start.3 = (s32[32,1]{0,1:T(1,128)S(1)}, s32[32,1]{0,1:T(1,128)}, u32[]{:S(2)}) copy-start(s32[32,1]{0,1:T(1,128)} %param.15) | copy-start | bytes 388
  14.0 2.7 %copy-start = (f32[24,64,128]{2,1,0:T(8,128)S(1)}, f32[24,64,128]{2,1,0:T(8,128)}, u32[]{:S(2)}) copy-start(f32[24,64,128]{2,1,0:T(8,128)} %section_ref.1) | copy-start | bytes 2359300
  14.0 2.7 %copy-start.1 = (f32[24,64,128]{2,1,0:T(8,128)S(1)}, f32[24,64,128]{2,1,0:T(8,128)}, u32[]{:S(2)}) copy-start(f32[24,64,128]{2,1,0:T(8,128)} %start_ref.1) | copy-start | bytes 2359300
  14.0 2.7 %copy-start.2 = (f32[2,64,128]{2,1,0:T(8,128)S(1)}, f32[2,64,128]{2,1,0:T(8,128)}, u32[]{:S(2)}) copy-start(f32[2,64,128]{2,1,0:T(8,128)} %velocity_ref.1) | copy-start | bytes 196612
  14.0 2.7 %copy-start.5 = (f32[24]{0:T(128)S(1)}, f32[24]{0:T(128)}, u32[]{:S(2)}) copy-start(f32[24]{0:T(128)} %spread_ref.1) | copy-start | bytes 292
  14.0 20.3 %copy-start.4 = (s32[1,128]{1,0:T(1,128)S(1)}, s32[1,128]{1,0:T(1,128)}, u32[]{:S(2)}) copy-start(s32[1,128]{1,0:T(1,128)} %cells_ref.1) | copy-start | bytes 1540

commit v3 on v2

--- a/solution.py
+++ b/solution.py
@@ -98,9 +98,9 @@
             (w_out_hbm, w_out_ref),
         )
     ):
-        copy = pltpu.make_async_copy(source, target, load_sem.at[k])
-        copy.start()
-        loads.append(copy)
+        loads.append(pltpu.make_async_copy(source, target, load_sem.at[k]))
+    loads[1].start()
+    loads[0].start()
     loads[1].wait()
     fields, rows_x, rows_y = section_ref.shape
     cells_x, cells_y = split_cells(cells_ref[...], rows_y)
@@ -108,6 +108,8 @@
     pick_y = (lax.broadcasted_iota(jnp.int32, (rows_y, count), 0) == cells_y).astype(F32)
     pick_x = row_mask(cells_x, rows_x)
     loads[0].wait()
+    for copy in loads[2:]:
+        copy.start()
     flat = section_ref[...].reshape(fields * rows_x, rows_y).astype(BF16)
     taken = jnp.dot(flat, pick_y.astype(BF16), preferred_element_type=F32)
     taken = taken.reshape(fields, rows_x, count)
@@ -357,7 +359,9 @@
         copy.wait_send()
 
 
-def update_kernel(cells_ref, rates_ref, base_ref, source_ref, new_ref):
+def update_kernel(
+    groups, cells_ref, rates_ref, base_ref, source_out, new_out, source_ref, new_ref, sems
+):
     fields, rows_x, rows_y = base_ref.shape
     cells_x, cells_y = split_cells(cells_ref[...], rows_y)
     count = cells_x.shape[1]
@@ -365,6 +369,8 @@
     pick_y = (lax.broadcasted_iota(jnp.int32, (rows_y, count), 0) == cells_y).astype(F32)
     pick_y = pick_y.astype(BF16)
     pick_y = jnp.concatenate([pick_y, pick_y], axis=1)
+    group = fields // groups
+    copies = []
     for f in range(fields):
         spread_rates = jnp.where(pick_x, rates_ref[f : f + 1, :], 0.0)
         top = spread_rates.astype(BF16)
@@ -377,6 +383,14 @@
         )
         source_ref[f] = source
         new_ref[f] = base_ref[f] + (0.25 * TIME_STEP) * source
+        if (f + 1) % group == 0:
+            span = pl.ds(f + 1 - group, group)
+            for k, (held, out) in enumerate(((source_ref, source_out), (new_ref, new_out))):
+                copy = pltpu.make_async_copy(held.at[span], out.at[span], sems.at[k, f // group])
+                copy.start()
+                copies.append(copy)
+    for copy in copies:
+        copy.wait()
 
 
 def whole(space=VMEM):
@@ -473,21 +487,20 @@
         ),
         name="giveback",
     )(team_of, diffusivity, slots, state_start, state_section, velocity, halo_x, halo_y)
-    step = 8 if fields % 8 == 0 else fields
-    tile = pl.BlockSpec((step, rows_x, rows_y), lambda i: (i, 0, 0))
+    groups = 6 if fields % 6 == 0 else fields
     return pl.pallas_call(
-        update_kernel,
-        grid=(fields // step,),
+        functools.partial(update_kernel, groups),
         out_shape=(
             jax.ShapeDtypeStruct(state_section.shape, F32),
             jax.ShapeDtypeStruct(state_section.shape, F32),
         ),
-        in_specs=[
-            pl.BlockSpec(flame_cells.shape, lambda i: (0, 0)),
-            pl.BlockSpec((step, count), lambda i: (i, 0)),
-            tile,
+        in_specs=[whole()] * 3,
+        out_specs=(whole(pl.ANY), whole(pl.ANY)),
+        scratch_shapes=[
+            VMEM(state_section.shape, F32),
+            VMEM(state_section.shape, F32),
+            dma((2, groups)),
         ],
-        out_specs=(tile, tile),
         compiler_params=pltpu.CompilerParams(vmem_limit_bytes=GRANT),
         name="update",
     )(flame_cells, rates, base)

time: 37.2 us -> 36.3 us (0.976)
  Pallas kernels: 35.7 us -> 35 us
    pallas_call x1, Pallas kernels: 2.22 us -> 1.5 us  [shards(): pl.pallas_call(functools.partial(update_kernel, groups), out_shape=(jax.S...]
where the time goes in v3:
time: 36.3 us; the launch traced here: 35.8 us
  Pallas kernels  35 us (96%)
  between operations  0.74 us (2%)
    pallas_call x1, Pallas kernels, shards(): pl.pallas_call(functools.partial(return_kernel, teams, members), out_shap...  17.6 us
    pallas_call x1, Pallas kernels, shards(): pl.pallas_call(functools.partial(share_kernel, teams, members), out_shape...  13.4 us
    pallas_call x1, Pallas kernels, shards(): pl.pallas_call(functools.partial(network_kernel, teams, members), out_sha...  2.61 us
    pallas_call x1, Pallas kernels, shards(): pl.pallas_call(functools.partial(update_kernel, groups), out_shape=(jax.S...  1.5 us

profile of v3, /device:TPU:0, one launch (start us, length us, event | category | flops | bytes accessed | tf_op | source)
XLA Modules:
  0.0 35.8 jit_solution(9810443993742254461)
XLA Ops:
  0.6 0.0 copy-start.3
  0.6 13.4 %share.1 = (bf16[4,8,24,128]{3,2,1,0:T(8,128)(2,1)S(1)}, bf16[2,24,128]{2,1,0:T(8,128)(2,1)S(1)}, bf16[2,64,128]{2,1,0:T(8,128)(2,1)S(1)}, bf16[1,1,1600,24]{3,2...) custom-call(f32[24,64,128]{2,1,0:T(8,128)} %section_ref.1, ...), custom_call_target="tpu_custom_call" | custom-call | tf_op jit(solution)/shard_map/share/pallas_call | solution.py:420
  14.0 0.0 copy-start
  14.0 0.0 copy-start.1
  14.0 0.0 copy-start.2
  14.0 0.0 copy-start.5
  14.1 0.0 copy-done.3
  14.1 0.0 copy-start.4
  14.1 2.6 %networks.1.slots_ref = f32[16,24,128]{2,1,0:T(8,128)S(1)} custom-call(s32[32]{0:T(128)S(1)} %bitcast.4, bf16[32,24,128]{2,1,0:T(8,128)(2,1)S(1)} %bitcast.3, bf16[1,1,1600,24]{3,2,1,0:T(8,128)(2,1)S(1)} %get-tuple-element.12.w_in, bf16[1,1,800,1600]{3,2,1,0:T(8,128)(2,1)S(1)} %get-tuple-element.13.w_mid, ...), custom_call_target="tpu_custom_call" | custom-call | tf_op jit(solution)/shard_map/networks/pallas_call | solution.py:453
  16.7 0.0 copy-done
  16.7 0.0 copy-done.1
  16.7 0.0 copy-done.2
  16.7 0.0 copy-done.5
  16.7 17.6 %giveback.1 = (f32[24,128]{1,0:T(8,128)S(1)}, f32[24,64,128]{2,1,0:T(8,128)S(1)}) custom-call(s32[32]{0:T(128)S(1)} %bitcast.5, f32[24]{0:T(128)S(1)} %copy-done.5, f32[16,24,128]{2,1,0:T(8,128)S(1)} %networks.1.slots_ref, f32[24,64,128]{2,1,0:T(8,128)S(1)} %copy-done.1, f32[24,64,128]{2,1,0:T(8,128)S(1)} %copy-done, f32[2,64,128]{2,1,0:T(8,128)S(1)} %copy-done.2, ...), custom_call_target="tpu_custom_call" | custom-call | tf_op jit(solution)/shard_map/giveback/pallas_call | solution.py:468
  34.3 0.0 copy-done.4
  34.3 1.5 %update.1 = (f32[24,64,128]{2,1,0:T(8,128)}, f32[24,64,128]{2,1,0:T(8,128)}) custom-call(s32[1,128]{1,0:T(1,128)S(1)} %copy-done.4, f32[24,128]{1,0:T(8,128)S(1)} %get-tuple-element.18.rates_ref, f32[24,64,128]{2,1,0:T(8,128)S(1)} %get-tuple-element.19.base_ref), custom_call_target="tpu_custom_call" | custom-call | tf_op jit(solution)/shard_map/update/pallas_call | solution.py:491
Async XLA Ops:
  0.6 13.4 %copy-start.3 = (s32[32,1]{0,1:T(1,128)S(1)}, s32[32,1]{0,1:T(1,128)}, u32[]{:S(2)}) copy-start(s32[32,1]{0,1:T(1,128)} %param.15) | copy-start | bytes 388
  14.0 2.7 %copy-start = (f32[24,64,128]{2,1,0:T(8,128)S(1)}, f32[24,64,128]{2,1,0:T(8,128)}, u32[]{:S(2)}) copy-start(f32[24,64,128]{2,1,0:T(8,128)} %section_ref.1) | copy-start | bytes 2359300
  14.0 2.7 %copy-start.1 = (f32[24,64,128]{2,1,0:T(8,128)S(1)}, f32[24,64,128]{2,1,0:T(8,128)}, u32[]{:S(2)}) copy-start(f32[24,64,128]{2,1,0:T(8,128)} %start_ref.1) | copy-start | bytes 2359300
  14.0 2.7 %copy-start.2 = (f32[2,64,128]{2,1,0:T(8,128)S(1)}, f32[2,64,128]{2,1,0:T(8,128)}, u32[]{:S(2)}) copy-start(f32[2,64,128]{2,1,0:T(8,128)} %velocity_ref.1) | copy-start | bytes 196612
  14.0 2.7 %copy-start.5 = (f32[24]{0:T(128)S(1)}, f32[24]{0:T(128)}, u32[]{:S(2)}) copy-start(f32[24]{0:T(128)} %spread_ref.1) | copy-start | bytes 292
  14.1 20.2 %copy-start.4 = (s32[1,128]{1,0:T(1,128)S(1)}, s32[1,128]{1,0:T(1,128)}, u32[]{:S(2)}) copy-start(s32[1,128]{1,0:T(1,128)} %cells_ref.1) | copy-start | bytes 1540
